TPU v7x, 32 devices: a whole 2x2x4 slice. The times are simulated.
32 devices in a mesh: dp: 16 (over z, x, core), mp: 2 (over y).
Axes of the slice: x: 2, y: 2, z: 4, core: 2. Of those that a mesh axis runs over, the one named last changes fastest.
Arguments:
- tokens: bfloat16 [16384, 1024], P('dp'), may hold values from -6 to 6
- page_lengths: int32 [32], P('dp'), may hold values from 64 to 512, as said below
- qkv_weight: bfloat16 [3, 1024, 1024], P(None, None, 'mp'), may hold values from -0.1875 to 0.1875
- qv_bias: bfloat16 [2, 1024], P(None, 'mp'), may hold values from -1.5 to 1.5
- out_weight: bfloat16 [1024, 1024], P('mp'), may hold values from -0.75 to 0.75
- out_bias: bfloat16 [1024], replicated, may hold values from -1.5 to 1.5
- ln1_gain: bfloat16 [1024], replicated, may hold values from 0.5 to 1.5
- ln1_bias: bfloat16 [1024], replicated, may hold values from -1.5 to 1.5
- ff1_weight: bfloat16 [1024, 4096], P(None, 'mp'), may hold values from -0.1875 to 0.1875
- ff1_bias: bfloat16 [4096], P('mp'), may hold values from -1.5 to 1.5
- ff2_weight: bfloat16 [4096, 1024], P('mp'), may hold values from -0.09375 to 0.09375
- ff2_bias: bfloat16 [1024], replicated, may hold values from -1.5 to 1.5
- ln2_gain: bfloat16 [1024], replicated, may hold values from 0.5 to 1.5
- ln2_bias: bfloat16 [1024], replicated, may hold values from -1.5 to 1.5
- cotangent: bfloat16 [16384, 1024], P('dp'), may hold values from -6 to 6
Outputs:
- out_rows: bfloat16 [16384, 1024], P(('dp', 'mp'))
- input_grad: bfloat16 [16384, 1024], P(('dp', 'mp'))
- qkv_weight_grad: float32 [3, 1024, 1024], P(None, 'dp', 'mp')
- qv_bias_grad: float32 [2, 1024], replicated
- out_weight_grad: float32 [1024, 1024], P('mp', 'dp')
- out_bias_grad: float32 [1024], replicated
- ln1_gain_grad: float32 [1024], replicated
- ln1_bias_grad: float32 [1024], replicated
- ff1_weight_grad: float32 [1024, 4096], P('dp', 'mp')
- ff1_bias_grad: float32 [4096], replicated
- ff2_weight_grad: float32 [4096, 1024], P('mp', 'dp')
- ff2_bias_grad: float32 [1024], replicated
- ln2_gain_grad: float32 [1024], replicated
- ln2_bias_grad: float32 [1024], replicated
Inputs may be any that keep to these rules, and one draw needn't show every extreme that they name: `page_lengths`: valid tokens of a page; some page has all 512 slots valid.
All inputs are finite; a program needn't handle non-finite values.
Results may differ from a plain program's by a relative error of at most 0.02.
Values may be sent and summed in bfloat16 or wider, within the bound.
No kernel may reach another device: no remote copies, remote signals or barrier semaphores. Data moves between devices by JAX's collectives and lax.ppermute only.
A program may use at most 192 MiB of HBM per device.

v0:
```python
import jax
import jax.numpy as jnp
from jax import lax
from jax.sharding import PartitionSpec as P

HD = 64


EPSILON = 1e-05
NEGATIVE = -1e30


def normalize(values):
    center = values - jnp.mean(values, axis=-1, keepdims=True)
    spread = jnp.mean(center * center, axis=-1, keepdims=True)
    return center * lax.rsqrt(spread + EPSILON)


def gelu_exact(values):
    return jax.nn.gelu(values, approximate=False)


def over_rows(left, right):
    return lax.dot_general(
        left, right, (((0,), (0,)), ((), ())), preferred_element_type=jnp.float32
    )


def over_cols(left, right):
    return lax.dot_general(
        left, right, (((1,), (1,)), ((), ())), preferred_element_type=jnp.float32
    )


def page_scores(query, keyset, valid):
    raw = jnp.einsum("qhe,khe->hqk", query, keyset, preferred_element_type=jnp.float32) * HD ** (
        -0.5
    )
    return jnp.where(valid[None, None, :], raw, NEGATIVE)


def attend(block):
    query, keyset, valueset, valid = block
    scores = page_scores(query, keyset, valid)
    top = jnp.max(scores, axis=-1, keepdims=True)
    expo = jnp.exp(scores - top)
    total = jnp.sum(expo, axis=-1, keepdims=True)
    probs = expo / total
    context = jnp.einsum(
        "hqk,khe->qhe", probs.astype(jnp.bfloat16), valueset, preferred_element_type=jnp.float32
    )
    context = context.astype(jnp.bfloat16)
    return (context.reshape(context.shape[0], -1), top[..., 0] + jnp.log(total[..., 0]))


def attend_back(block):
    query, keyset, valueset, valid, logsum, dcontext = block
    scale = HD ** (-0.5)
    scores = page_scores(query, keyset, valid)
    probs = jnp.exp(scores - logsum[..., None])
    dprobs = jnp.einsum("qhe,khe->hqk", dcontext, valueset, preferred_element_type=jnp.float32)
    delta = jnp.sum(probs * dprobs, axis=-1, keepdims=True)
    dscores = (probs * (dprobs - delta)).astype(jnp.bfloat16)
    dquery = (
        jnp.einsum("hqk,khe->qhe", dscores, keyset, preferred_element_type=jnp.float32) * scale
    ).astype(jnp.bfloat16)
    dkeys = (
        jnp.einsum("hqk,qhe->khe", dscores, query, preferred_element_type=jnp.float32) * scale
    ).astype(jnp.bfloat16)
    dvalues = jnp.einsum(
        "hqk,qhe->khe", probs.astype(jnp.bfloat16), dcontext, preferred_element_type=jnp.float32
    ).astype(jnp.bfloat16)
    seq_len = query.shape[0]
    return (dquery.reshape(seq_len, -1), dkeys.reshape(seq_len, -1), dvalues.reshape(seq_len, -1))


def local(
    tokens,
    page_lengths,
    qkv_weight,
    qv_bias,
    out_weight,
    out_bias,
    ln1_gain,
    ln1_bias,
    ff1_weight,
    ff1_bias,
    ff2_weight,
    ff2_bias,
    ln2_gain,
    ln2_bias,
    cotangent,
):
    row_count = tokens.shape[0]
    page_count = page_lengths.shape[0]
    seq_len = row_count // page_count
    cols = qkv_weight.shape[2]
    ff_cols = ff1_weight.shape[1]
    group_heads = cols // HD
    share = row_count // lax.axis_size("mp")
    group = lax.axis_index("mp")
    share_start = group * share
    gain_one = ln1_gain.astype(jnp.float32)
    shift_one = ln1_bias.astype(jnp.float32)
    gain_two = ln2_gain.astype(jnp.float32)
    shift_two = ln2_bias.astype(jnp.float32)

    def own_rows(values):
        return lax.dynamic_slice_in_dim(values, share_start, share, 0)

    projected = jnp.einsum("rd,tdc->trc", tokens, qkv_weight, preferred_element_type=jnp.float32)
    bias_rows = jnp.stack([qv_bias[0], jnp.zeros_like(qv_bias[0]), qv_bias[1]]).astype(jnp.float32)
    qkv_rows = (projected + bias_rows[:, None, :]).astype(jnp.bfloat16)
    qkv_pages = qkv_rows.reshape(3, page_count, seq_len, group_heads, HD)
    valid = jnp.arange(seq_len)[None, :] < page_lengths[:, None]
    context, logsum = lax.map(attend, (qkv_pages[0], qkv_pages[1], qkv_pages[2], valid))
    context = context.reshape(row_count, cols)
    attn_part = jnp.dot(context, out_weight, preferred_element_type=jnp.float32).astype(
        jnp.bfloat16
    )
    attn = lax.psum(attn_part, "mp").astype(jnp.float32)
    first_sum = tokens.astype(jnp.float32) + attn + out_bias.astype(jnp.float32)
    normed_one, norm_one_back = jax.vjp(normalize, first_sum)
    hidden = normed_one * gain_one + shift_one
    hidden_low = hidden.astype(jnp.bfloat16)
    normed_one_own = own_rows(normed_one)
    pre = jnp.dot(hidden_low, ff1_weight, preferred_element_type=jnp.float32) + ff1_bias.astype(
        jnp.float32
    )
    activated, gelu_back = jax.vjp(gelu_exact, pre)
    act_low = activated.astype(jnp.bfloat16)
    ffn_part = jnp.dot(act_low, ff2_weight, preferred_element_type=jnp.float32).astype(jnp.bfloat16)
    cot_own = own_rows(cotangent).astype(jnp.float32)
    ffn = lax.psum(ffn_part, "mp").astype(jnp.float32)
    second_sum = hidden + ffn + ff2_bias.astype(jnp.float32)
    normed_two, norm_two_back = jax.vjp(normalize, second_sum)
    normed_two_own = own_rows(normed_two)
    out_rows = (normed_two_own * gain_two + shift_two).astype(jnp.bfloat16)
    dsecond = norm_two_back(cotangent.astype(jnp.float32) * gain_two)[0]
    dffn = dsecond.astype(jnp.bfloat16)
    dsecond_own = own_rows(dsecond)
    dgain_two = jnp.sum(cot_own * normed_two_own, axis=0)
    dshift_two = jnp.sum(cot_own, axis=0)
    dff2_bias = jnp.sum(dsecond_own, axis=0)
    dff2_weight = over_rows(act_low, dffn)
    dact = over_cols(dffn, ff2_weight)
    dpre = gelu_back(dact)[0].astype(jnp.bfloat16)
    dff1_bias = jnp.sum(dpre.astype(jnp.float32), axis=0)
    dff1_weight = over_rows(hidden_low, dpre)
    dhid_part = over_cols(dpre, ff1_weight).astype(jnp.bfloat16)
    dhidden = dsecond + lax.psum(dhid_part, "mp").astype(jnp.float32)
    dfirst = norm_one_back(dhidden * gain_one)[0]
    dattn = dfirst.astype(jnp.bfloat16)
    dhidden_own = own_rows(dhidden)
    dfirst_own = own_rows(dfirst)
    dgain_one = jnp.sum(dhidden_own * normed_one_own, axis=0)
    dshift_one = jnp.sum(dhidden_own, axis=0)
    dout_bias = jnp.sum(dfirst_own, axis=0)
    dout_weight = over_rows(context, dattn)
    dcontext = over_cols(dattn, out_weight).astype(jnp.bfloat16)
    dcontext_pages = dcontext.reshape(page_count, seq_len, group_heads, HD)
    dquery, dkeys, dvalues = lax.map(
        attend_back, (qkv_pages[0], qkv_pages[1], qkv_pages[2], valid, logsum, dcontext_pages)
    )
    dqkv = jnp.stack(
        [
            dquery.reshape(row_count, cols),
            dkeys.reshape(row_count, cols),
            dvalues.reshape(row_count, cols),
        ]
    )
    dqv_bias = jnp.stack(
        [jnp.sum(dqkv[0].astype(jnp.float32), axis=0), jnp.sum(dqkv[2].astype(jnp.float32), axis=0)]
    )
    dqkv_weight = jnp.einsum("rd,trc->tdc", tokens, dqkv, preferred_element_type=jnp.float32)
    dtok_part = jnp.einsum(
        "trc,tdc->rd", dqkv, qkv_weight, preferred_element_type=jnp.float32
    ).astype(jnp.bfloat16)
    input_grad = (
        dfirst_own
        + lax.psum_scatter(dtok_part, "mp", scatter_dimension=0, tiled=True).astype(jnp.float32)
    ).astype(jnp.bfloat16)
    qkv_share, out_share, ff1_share, ff2_share = (
        lax.psum_scatter(
            dqkv_weight.astype(jnp.bfloat16), "dp", scatter_dimension=1, tiled=True
        ).astype(jnp.float32),
        lax.psum_scatter(
            dout_weight.astype(jnp.bfloat16), "dp", scatter_dimension=1, tiled=True
        ).astype(jnp.float32),
        lax.psum_scatter(
            dff1_weight.astype(jnp.bfloat16), "dp", scatter_dimension=0, tiled=True
        ).astype(jnp.float32),
        lax.psum_scatter(
            dff2_weight.astype(jnp.bfloat16), "dp", scatter_dimension=1, tiled=True
        ).astype(jnp.float32),
    )
    qv_placed = lax.dynamic_update_slice_in_dim(
        jnp.zeros((2, cols * lax.axis_size("mp")), jnp.float32), dqv_bias, group * cols, 1
    )
    ff1_placed = lax.dynamic_update_slice_in_dim(
        jnp.zeros((ff_cols * lax.axis_size("mp"),), jnp.float32), dff1_bias, group * ff_cols, 0
    )
    small = lax.psum(
        (qv_placed, dout_bias, dgain_one, dshift_one, ff1_placed, dff2_bias, dgain_two, dshift_two),
        ("dp", "mp"),
    )
    return (
        out_rows,
        input_grad,
        qkv_share,
        small[0],
        out_share,
        small[1],
        small[2],
        small[3],
        ff1_share,
        small[4],
        ff2_share,
        small[5],
        small[6],
        small[7],
    )


def solution(mesh):
    in_specs = (
        P("dp", None),
        P("dp"),
        P(None, None, "mp"),
        P(None, "mp"),
        P("mp", None),
        P(),
        P(),
        P(),
        P(None, "mp"),
        P("mp"),
        P("mp", None),
        P(),
        P(),
        P(),
        P("dp", None),
    )
    out_specs = (
        P(("dp", "mp"), None),
        P(("dp", "mp"), None),
        P(None, "dp", "mp"),
        P(),
        P("mp", "dp"),
        P(),
        P(),
        P(),
        P("dp", "mp"),
        P(),
        P("mp", "dp"),
        P(),
        P(),
        P(),
    )
    return jax.shard_map(local, mesh=mesh, in_specs=in_specs, out_specs=out_specs, check_vma=False)
```

profile of v0, /device:TPU:0, one launch (start us, length us, event | category | flops | bytes accessed | tf_op | source)
XLA Modules:
  0.0 775.8 jit_solution(8002461027185806768)
XLA Ops:
  9.1 5.5 fusion.56
  16.3 2.6 squeeze.41
  18.9 2.4 copy.72
  21.4 2.6 squeeze.40
  24.0 2.4 copy.71
  26.4 2.6 squeeze.39
  32.4 24.3 %while.26 = (s32[]{:T(128)}, bf16[2,512,512]{2,1,0:T(8,128)(2,1)}, f32[2,8,512]{2,1,0:T(8,128)S(1)}, bf16[2,512,8,64]{1,3,2,0:T(8,128)(2,1)}, pred[2,512]{1,0:T(...) while((s32[]{:T(128)}, bf16[2,512,512]{2,1,0:T(8,128)(2,1)}, ...), condition=%wide.region_3.4_spmd, body=%wide.region_0.3_spmd.sunk | while | flops 562294784 | bytes 33689224 | solution.py:116
  32.5 3.1 fusion.115
  37.6 3.0 fusion.117
  44.6 3.1 fusion.115
  49.8 3.0 fusion.117
  56.7 4.2 convolution_convert_fusion.4
  61.3 65.4 %all-reduce.7.cloned.1.call-done = bf16[1024,1024]{1,0:T(8,128)(2,1)} async-done(((bf16[1024,1024]{1,0:T(8,128)(2,1)}), bf16[1024,1024]{1,0:T(8,128)(2,1)}) %all-reduce.7.cloned.1.call-update) | async-done | bytes 2097168 | tf_op jit(solution)/shard_map/psum | solution.py:121
  126.7 3.1 fusion.54
  133.5 24.4 %multiply_convert_fusion.1 = (bf16[1024,2048]{1,0:T(8,128)(2,1)S(1)}, f32[1024,2048]{1,0:T(8,128)}, f32[1024,2048]{1,0:T(8,128)}) fusion(f32[2048]{0:T(1024)S(1)} %convert_element_type.172, bf16[1024,2048]{1,0:T(8,128)(2,1)S(1)} %copy-done.36, f32[1024,1024]{1,0:T(8,128)S(1)} %broadcast_multiply_fusion, f32[1024]{0:T(1024)S(1)} %convert_element_type.170, ...), kind=kOutput, calls=%fused_computation.64 | convolution fusion | flops 4436525056 | bytes 29376512 | tf_op jit(solution)/shard_map/dot_general | solution.py:127
  159.9 5.7 convolution_convert_fusion.3
  166.2 62.6 %all-reduce.9.cloned.1.call-done = bf16[1024,1024]{1,0:T(8,128)(2,1)} async-done(((bf16[1024,1024]{1,0:T(8,128)(2,1)}), bf16[1024,1024]{1,0:T(8,128)(2,1)}) %all-reduce.9.cloned.1.call-update) | async-done | bytes 2097168 | tf_op jit(solution)/shard_map/psum | solution.py:134
  228.8 3.9 fusion.58
  233.5 3.5 multiply_reduce_fusion.2
  241.1 13.0 %convert_reduce_fusion = (f32[2048]{0:T(1024)}, bf16[1024,2048]{1,0:T(8,128)(2,1)}) fusion(f32[1024,2048]{1,0:T(8,128)} %get-tuple-element.258, bf16[2048,1024]{1,0:T(8,128)(2,1)S(1)} %copy-done.35, f32[1024,1024]{1,0:T(8,128)S(1)} %broadcast_add_fusion.1, f32[1024,2048]{1,0:T(8,128)} %get-tuple-element.275, f32[2048]{0:T(1024)S(1)} %convert_element_type.172), kind=kOutput, calls=%fused_computation.62 | convolution fusion | flops 4331665408 | bytes 29376512 | tf_op jit(solution)/shard_map/dot_general | solution.py:30
  254.1 8.0 %convolution_convert_fusion.2 = bf16[1024,1024]{1,0:T(8,128)(2,1)} fusion(bf16[1024,2048]{1,0:T(8,128)(2,1)} %get-tuple-element.277, bf16[1024,2048]{1,0:T(8,128)(2,1)S(1)} %copy-done.37), kind=kOutput, calls=%fused_computation.118 | convolution fusion | flops 4296015872 | bytes 10485760 | tf_op jit(solution)/shard_map/dot_general | solution.py:30
  262.2 63.0 %all-reduce.11.cloned.1.call-done = bf16[1024,1024]{1,0:T(8,128)(2,1)} async-done(((bf16[1024,1024]{1,0:T(8,128)(2,1)}), bf16[1024,1024]{1,0:T(8,128)(2,1)}) %all-reduce.11.cloned.1.call-update) | async-done | bytes 2097168 | tf_op jit(solution)/shard_map/psum | solution.py:151
  325.2 5.7 multiply_reduce_fusion.1
  337.9 3.9 reshape.153
  341.8 3.3 copy.77
  346.2 42.9 %while.27 = (s32[]{:T(128)}, bf16[2,512,512]{1,2,0:T(8,128)(2,1)}, bf16[2,512,512]{2,1,0:T(8,128)(2,1)}, bf16[2,512,512]{1,2,0:T(8,128)(2,1)}, bf16[2,512,8,64]{...) while((s32[]{:T(128)}, bf16[2,512,512]{1,2,0:T(8,128)(2,1)}, ...), condition=%wide.region_17.18_spmd, body=%wide.region_15.17_spmd.sunk | while | flops 1374941184 | bytes 89248512 | solution.py:162
  346.2 2.6 fusion.126
  348.8 2.9 fusion.127
  351.8 3.0 multiply_reduce_fusion.7
  354.7 2.8 multiply_convert_fusion.3
  367.6 2.6 fusion.126
  370.2 2.9 fusion.127
  373.1 3.0 multiply_reduce_fusion.7
  376.1 2.8 multiply_convert_fusion.3
  393.7 7.7 convert_bitcast_fusion
  401.4 7.7 copy.83
  409.1 4.8 convolution_convert_fusion.5
  414.0 10.2 %convolution_convert_fusion = bf16[2048,1024]{0,1:T(8,128)(2,1)} fusion(bf16[1024,2048]{1,0:T(8,128)(2,1)} %copy-done.40, f32[1024,1024]{1,0:T(8,128)} %copy-done.11), kind=kOutput, calls=%fused_computation.91 | convolution fusion | flops 4298113024 | bytes 12582912 | tf_op jit(solution)/shard_map/dot_general | solution.py:24
  424.3 6.6 bitcast_convert_fusion
  431.3 10.2 %convolution_convert_fusion.1 = bf16[1024,2048]{1,0:T(8,128)(2,1)} fusion(bf16[1024,2048]{1,0:T(8,128)(2,1)} %get-tuple-element.277, f32[1024,1024]{1,0:T(8,128)} %copy-done.7, f32[1024]{0:T(1024)S(1)} %copy-done.25, f32[1024]{0:T(1024)S(1)} %convert_element_type.169), kind=kOutput, calls=%fused_computation.92 | convolution fusion | flops 4300210176 | bytes 12591104 | tf_op jit(solution)/shard_map/dot_general | solution.py:24
  445.8 3.6 convert_reduce_fusion.1
  452.0 68.8 %all-reduce.13.cloned.1.call-done = bf16[3,1024,512]{2,0,1:T(4,128)(2,1)} async-done(((bf16[3,1024,512]{2,0,1:T(4,128)(2,1)}), bf16[3,1024,512]{2,0,1:T(4,128)(2,1)}) %all-reduce.13.cloned.1.call-update) | async-done | bytes 3145744
  522.7 57.9 %reduce-scatter.7.cloned.1.call-done = bf16[512,64]{0,1:T(8,128)(2,1)} async-done(((bf16[512,1024]{0,1:T(8,128)(2,1)}), bf16[512,64]{0,1:T(8,128)(2,1)}) %reduce-scatter.7.cloned.1.call-update) | async-done | bytes 65552 | tf_op jit(solution)/shard_map/reduce_scatter | solution.py:187
  582.1 74.2 %reduce-scatter.11.cloned.1.call-done = bf16[2048,64]{0,1:T(8,128)(2,1)} async-done(((bf16[2048,1024]{0,1:T(8,128)(2,1)}), bf16[2048,64]{0,1:T(8,128)(2,1)}) %reduce-scatter.11.cloned.1.call-update) | async-done | bytes 262160 | tf_op jit(solution)/shard_map/reduce_scatter | solution.py:193
  658.1 31.3 %reduce-scatter.5.cloned.1.call-done = bf16[512,1024]{1,0:T(8,128)(2,1)} async-done(((bf16[1024,1024]{1,0:T(8,128)(2,1)}), bf16[512,1024]{1,0:T(8,128)(2,1)}) %reduce-scatter.5.cloned.1.call-update) | async-done | bytes 1048592 | tf_op jit(solution)/shard_map/reduce_scatter | solution.py:181
  689.4 3.2 dynamic-slice_reduce_fusion.4
  692.6 40.9 %all-reduce.1 = (f32[2,1024]{1,0:T(2,128)}, f32[1024]{0:T(1024)}, f32[1024]{0:T(1024)}, f32[1024]{0:T(1024)}, f32[4096]{0:T(1024)}, /*index=5*/f32[1024]{0:T(1024)}, f32[1024]{0:T(1024)}, f32[1024]{0:T(1024)}) all-reduce(f32[2,1024]{1,0:T(2,128)S(1)} %maximum_dynamic-update-slice_fusion, ...), channel_id=1, replica_groups=mesh['dp'=16,'mp'=2] {'dp','mp'}, use_global_device_ids=true, to_apply=%region_22.23 | all-reduce | flops 12288 | bytes 98304 | tf_op jit(solution)/shard_map/psum | solution.py:203
  733.5 33.2 %reduce-scatter.9.cloned.1.call-done = bf16[64,2048]{1,0:T(8,128)(2,1)} async-done(((bf16[1024,2048]{1,0:T(8,128)(2,1)}), bf16[64,2048]{1,0:T(8,128)(2,1)}) %reduce-scatter.9.cloned.1.call-update) | async-done | bytes 262160 | tf_op jit(solution)/shard_map/reduce_scatter | solution.py:190
  (180 shorter events, 76.3 us)
Async XLA Ops:
  7.2 119.5 %all-reduce.7.cloned.1.call-start = ((), (), s32[]{:S(2)}) async-start(), calls=%async_computation.4 | async-start | bytes 4194304 | tf_op jit(solution)/shard_map/psum | solution.py:121
  35.6 2.0 copy-start.15
  56.7 4.5 copy-start.28
  56.7 4.5 copy-start.29
  56.7 4.5 copy-start.30
  56.7 4.6 copy-start.27
  60.9 167.8 %all-reduce.9.cloned.1.call-start = ((), (), s32[]{:S(2)}) async-start(), calls=%async_computation.5 | async-start | bytes 4194304 | tf_op jit(solution)/shard_map/psum | solution.py:134
  61.3 171.4 %copy-start.24 = (f32[1024]{0:T(1024)}, f32[1024]{0:T(1024)S(1)}, u32[]{:S(2)}) copy-start(f32[1024]{0:T(1024)S(1)} %convert_element_type.170) | copy-start | bytes 12292
  126.7 3.1 copy-start.3
  126.7 3.5 copy-start.5
  131.3 2.2 copy-start.36
  133.4 24.4 %copy-start.7 = (f32[1024,1024]{1,0:T(8,128)}, f32[1024,1024]{1,0:T(8,128)S(1)}, u32[]{:S(2)}) copy-start(f32[1024,1024]{1,0:T(8,128)S(1)} %broadcast_multiply_fusion) | copy-start | bytes 12582916
  133.5 26.5 %copy-start.34 = (bf16[2048,1024]{1,0:T(8,128)(2,1)S(1)}, bf16[2048,1024]{1,0:T(8,128)(2,1)}, u32[]{:S(2)}) copy-start(bf16[2048,1024]{1,0:T(8,128)(2,1)} %param.29) | copy-start | bytes 12582916
  157.9 2.0 copy-start.40
  159.9 6.2 copy-start.31
  159.9 6.2 copy-start.32
  165.7 159.5 %all-reduce.11.cloned.1.call-start = ((), (), s32[]{:S(2)}) async-start(), calls=%async_computation.6 | async-start | bytes 4194304 | tf_op jit(solution)/shard_map/psum | solution.py:151
  166.2 72.0 %copy-start.20 = (f32[1024]{0:T(1024)}, f32[1024]{0:T(1024)S(1)}, u32[]{:S(2)}) copy-start(f32[1024]{0:T(1024)S(1)} %convert_element_type.177) | copy-start | bytes 12292
  228.8 4.0 copy-start.8
  228.8 4.7 copy-start.13
  237.0 2.4 copy-start.10
  237.0 2.4 copy-start.22
  238.2 3.0 copy-start.35
  239.4 14.7 %copy-start.11 = (f32[1024,1024]{1,0:T(8,128)}, f32[1024,1024]{1,0:T(8,128)S(1)}, u32[]{:S(2)}) copy-start(f32[1024,1024]{1,0:T(8,128)S(1)} %broadcast_add_fusion.1) | copy-start | bytes 12582916
  241.1 13.0 %copy-start.37 = (bf16[1024,2048]{1,0:T(8,128)(2,1)S(1)}, bf16[1024,2048]{1,0:T(8,128)(2,1)}, u32[]{:S(2)}) copy-start(bf16[1024,2048]{1,0:T(8,128)(2,1)} %param.27) | copy-start | bytes 12582916
  262.1 258.7 %all-reduce.13.cloned.1.call-start = ((), (), s32[]{:S(2)}) async-start(), calls=%async_computation.11 | async-start | bytes 8388608
  325.2 5.8 copy-start.4
  325.2 5.8 copy-start.6
  330.9 2.4 copy-start.12
  333.4 2.3 copy-start.38
  346.2 2.6 copy-start.14
  348.8 2.9 copy-start.16
  354.7 2.9 copy-start.2
  357.6 2.2 copy-start.1
  367.6 2.6 copy-start.14
  370.2 2.9 copy-start.16
  376.1 2.9 copy-start.2
  379.0 2.2 copy-start.1
  409.1 171.5 %reduce-scatter.7.cloned.1.call-start = ((), (), s32[]{:S(2)}) async-start(), calls=%async_computation.8 | async-start | bytes 1114112 | tf_op jit(solution)/shard_map/reduce_scatter | solution.py:187
  414.0 242.3 %reduce-scatter.11.cloned.1.call-start = ((), (), s32[]{:S(2)}) async-start(), calls=%async_computation.10 | async-start | bytes 4456448 | tf_op jit(solution)/shard_map/reduce_scatter | solution.py:193
  424.3 7.0 copy-start.25
  424.3 265.1 %reduce-scatter.5.cloned.1.call-start = ((), (), s32[]{:S(2)}) async-start(), calls=%async_computation.7 | async-start | bytes 3145728 | tf_op jit(solution)/shard_map/reduce_scatter | solution.py:181
  431.0 335.8 %reduce-scatter.9.cloned.1.call-start = ((), (), s32[]{:S(2)}) async-start(), calls=%async_computation.9 | async-start | bytes 4456448 | tf_op jit(solution)/shard_map/reduce_scatter | solution.py:190
  441.5 2.0 copy-start.26
  441.5 4.3 copy-start.21
  443.4 6.0 copy-start.9
  445.8 5.8 copy-start.18
  445.8 5.8 copy-start.19
  (6 other events, 9.1 us)
Sparse Core Ops, SparseCore 0:
  61.1 65.5 all-reduce.6
  165.8 62.9 all-reduce.8
  262.2 62.9 all-reduce.10
  409.2 111.5 all-reduce.12
  524.3 56.2 reduce-scatter.6
  584.8 71.4 reduce-scatter.10
  658.5 30.8 reduce-scatter.4
  693.8 72.9 reduce-scatter.8
where the time goes:
time: 785 us; the launch traced here: 776 us
  waiting for transfers between devices  457 us (58%)
  matrix products  139 us (18%)
  local copies, waits for them, and re-layouts  70.2 us (9%)
  other arithmetic  51.3 us (7%)
  blocking collectives  40.9 us (5%)
  between operations  15.7 us (2%)
    reduce_scatter x1, waiting for transfers between devices, local(): lax.psum_scatter(dff2_weight.astype(jnp.bfloat16), 'dp', scatter_dimensio...  74.2 us
    unnamed x9, waiting for transfers between devices  68.9 us
    psum x1, waiting for transfers between devices, local(): attn = lax.psum(attn_part, 'mp').astype(jnp.float32)  65.4 us
    psum x1, waiting for transfers between devices, local(): dhidden = dsecond + lax.psum(dhid_part, 'mp').astype(jnp.float32)  63 us
    psum x1, waiting for transfers between devices, local(): ffn = lax.psum(ffn_part, 'mp').astype(jnp.float32)  62.6 us
    reduce_scatter x1, waiting for transfers between devices, local(): lax.psum_scatter(dout_weight.astype(jnp.bfloat16), 'dp', scatter_dimensio...  57.9 us
    psum x1, blocking collectives, local(): lax.psum((qv_placed, dout_bias, dgain_one, dshift_one, ff1_placed, dff2_b...  40.9 us
    reduce_scatter x1, waiting for transfers between devices, local(): lax.psum_scatter(dff1_weight.astype(jnp.bfloat16), 'dp', scatter_dimensio...  33.2 us
  transfers between devices with their start and end apart: 8, of which 8 were waited for; matrix products, arithmetic and copies ran while one was open for 6% of the time, Pallas kernels for 0%

commit v1 on v0

--- a/solution.py
+++ b/solution.py
@@ -1,6 +1,10 @@
+import functools
+
 import jax
 import jax.numpy as jnp
 from jax import lax
+from jax.experimental import pallas as pl
+from jax.experimental.pallas import tpu as pltpu
 from jax.sharding import PartitionSpec as P
 
 HD = 64
@@ -222,6 +226,430 @@
     )
 
 
+BF = jnp.bfloat16
+F32 = jnp.float32
+
+
+def dg(left, right, left_dim, right_dim):
+    return lax.dot_general(
+        left, right, (((left_dim,), (right_dim,)), ((), ())), preferred_element_type=F32
+    )
+
+
+def attn_fwd_body(len_ref, q_ref, k_ref, v_ref, ctx_ref, lse_ref, *, seq):
+    count = len_ref[pl.program_id(0)]
+    query = q_ref[...] * BF(HD**-0.5)
+    keyset = k_ref[...]
+    turned = v_ref[...].T
+    first = lax.broadcasted_iota(jnp.int32, query.shape, 1) < HD
+    keep = lax.broadcasted_iota(jnp.int32, (seq, seq), 0) < count
+    outs = []
+    for h in range(2):
+        own = jnp.where(first if h == 0 else ~first, query, BF(0))
+        scores = jnp.where(keep, dg(keyset, own, 1, 1), NEGATIVE)
+        top = jnp.max(scores, axis=0, keepdims=True)
+        expo = jnp.exp(scores - top)
+        total = jnp.sum(expo, axis=0, keepdims=True)
+        part = dg(turned[h * HD : (h + 1) * HD], expo.astype(BF), 1, 0)
+        outs.append(part * (1.0 / total))
+        lse_ref[0, 0, h : h + 1, :] = top + jnp.log(total)
+    ctx_ref[...] = jnp.concatenate(outs, axis=0).T.astype(BF)
+
+
+def attn_fwd(lengths, query, keyset, valueset):
+    rows, cols = query.shape
+    pages = lengths.shape[0]
+    seq = rows // pages
+    pairs = cols // (2 * HD)
+    spec = pl.BlockSpec((seq, 2 * HD), lambda p, j, n: (p, j))
+    return pl.pallas_call(
+        functools.partial(attn_fwd_body, seq=seq),
+        out_shape=(
+            jax.ShapeDtypeStruct((rows, cols), BF),
+            jax.ShapeDtypeStruct((pages, pairs, 2, seq), F32),
+        ),
+        grid_spec=pltpu.PrefetchScalarGridSpec(
+            num_scalar_prefetch=1,
+            grid=(pages, pairs),
+            in_specs=[spec] * 3,
+            out_specs=[spec, pl.BlockSpec((1, 1, 2, seq), lambda p, j, n: (p, j, 0, 0))],
+        ),
+        cost_estimate=pl.CostEstimate(
+            flops=16 * rows * seq * cols,
+            bytes_accessed=rows * cols * 8,
+            transcendentals=rows * seq * cols // HD,
+        ),
+        name="attn_fwd",
+    )(lengths, query, keyset, valueset)
+
+
+def attn_bwd_body(
+    len_ref, q_ref, k_ref, v_ref, lse_ref, dc_ref, dq_ref, dk_ref, dv_ref, *, seq
+):
+    count = len_ref[pl.program_id(0)]
+    query = q_ref[...] * BF(HD**-0.5)
+    keyset = k_ref[...]
+    valueset = v_ref[...]
+    dctx = dc_ref[...]
+    first = lax.broadcasted_iota(jnp.int32, query.shape, 1) < HD
+    keep = lax.broadcasted_iota(jnp.int32, (seq, seq), 0) < count
+    dquery = dkeys = dvalues = 0.0
+    for h in range(2):
+        mask = first if h == 0 else ~first
+        q_own = jnp.where(mask, query, BF(0))
+        k_own = jnp.where(mask, keyset, BF(0))
+        dc_own = jnp.where(mask, dctx, BF(0))
+        scores = dg(keyset, q_own, 1, 1) - lse_ref[0, 0, h : h + 1, :]
+        probs = jnp.exp(jnp.where(keep, scores, NEGATIVE))
+        dprobs = dg(valueset, dc_own, 1, 1)
+        delta = jnp.sum(probs * dprobs, axis=0, keepdims=True)
+        dscores = (probs * (dprobs - delta)).astype(BF)
+        dvalues = dvalues + dg(probs.astype(BF), dc_own, 1, 0)
+        dkeys = dkeys + dg(dscores, q_own, 1, 0)
+        dquery = dquery + dg(dscores, k_own, 0, 0)
+    dq_ref[...] = (dquery * HD**-0.5).astype(BF)
+    dk_ref[...] = dkeys.astype(BF)
+    dv_ref[...] = dvalues.astype(BF)
+
+
+def attn_bwd(lengths, query, keyset, valueset, logsum, dctx):
+    rows, cols = query.shape
+    pages = lengths.shape[0]
+    seq = rows // pages
+    pairs = cols // (2 * HD)
+    spec = pl.BlockSpec((seq, 2 * HD), lambda p, j, n: (p, j))
+    return pl.pallas_call(
+        functools.partial(attn_bwd_body, seq=seq),
+        out_shape=(jax.ShapeDtypeStruct((rows, cols), BF),) * 3,
+        grid_spec=pltpu.PrefetchScalarGridSpec(
+            num_scalar_prefetch=1,
+            grid=(pages, pairs),
+            in_specs=[spec] * 3
+            + [pl.BlockSpec((1, 1, 2, seq), lambda p, j, n: (p, j, 0, 0)), spec],
+            out_specs=[spec] * 3,
+        ),
+        cost_estimate=pl.CostEstimate(
+            flops=40 * rows * seq * cols,
+            bytes_accessed=rows * cols * 14,
+            transcendentals=rows * seq * cols // HD,
+        ),
+        name="attn_bwd",
+    )(lengths, query, keyset, valueset, logsum, dctx)
+
+
+def ff1_body(h_ref, w_ref, b_ref, act_ref, slope_ref):
+    pre = dg(h_ref[...], w_ref[...], 1, 0) + b_ref[...].astype(F32)
+    phi = 0.5 + 0.5 * lax.erf(pre * F32(2**-0.5))
+    act_ref[...] = (pre * phi).astype(BF)
+    density = jnp.exp(-0.5 * pre * pre) * F32(0.3989422804014327)
+    slope_ref[...] = (phi + pre * density).astype(BF)
+
+
+def ff1_gelu(hidden, weight, bias):
+    rows, depth = hidden.shape
+    units = weight.shape[1]
+    tile = min(512, units)
+    return pl.pallas_call(
+        ff1_body,
+        out_shape=(jax.ShapeDtypeStruct((rows, units), BF),) * 2,
+        grid=(units // tile,),
+        in_specs=[
+            pl.BlockSpec((rows, depth), lambda j: (0, 0)),
+            pl.BlockSpec((depth, tile), lambda j: (0, j)),
+            pl.BlockSpec((1, tile), lambda j: (0, j)),
+        ],
+        out_specs=[pl.BlockSpec((rows, tile), lambda j: (0, j))] * 2,
+        cost_estimate=pl.CostEstimate(
+            flops=2 * rows * depth * units,
+            bytes_accessed=2 * (rows * depth + depth * units + 2 * rows * units),
+            transcendentals=2 * rows * units,
+        ),
+        name="ff1_gelu",
+    )(hidden, weight, bias.reshape(1, units))
+
+
+def swap(values, bit):
+    count = lax.axis_size("dp")
+    return lax.ppermute(values, "dp", [(i, i ^ (1 << bit)) for i in range(count)])
+
+
+def swap_y(values):
+    return lax.ppermute(values, "mp", [(0, 1), (1, 0)])
+
+
+def place_body(me_ref, *refs, offsets):
+    pieces = refs[: len(offsets)]
+    out = refs[len(offsets)]
+    for piece, (rel, start, size) in zip(pieces, offsets):
+        at = pl.multiple_of(((me_ref[0] ^ rel) & 7) * size + start, 16)
+        out[pl.ds(at, piece.shape[0]), :] = piece[...]
+
+
+def gather_other(weight, me):
+    rows, cols = weight.shape
+    size = rows // 8
+    half = size // 2
+    mine = swap_y(lax.dynamic_slice_in_dim(weight, (me & 7) * size, size, 0))
+    by_x = swap(mine, 1)
+    by_z = swap(mine, 2)
+    low = swap(by_z[:half], 1)
+    high = swap(by_x[half:], 2)
+    near = [(0, 0, mine), (2, 0, by_x), (4, 0, by_z), (6, 0, low), (6, half, high)]
+    pieces = near + [(rel ^ 1, start, swap(piece, 0)) for rel, start, piece in near]
+    offsets = tuple((rel, start, size) for rel, start, _ in pieces)
+    tile = min(256, cols)
+    return pl.pallas_call(
+        functools.partial(place_body, offsets=offsets),
+        out_shape=jax.ShapeDtypeStruct((rows, cols), weight.dtype),
+        grid_spec=pltpu.PrefetchScalarGridSpec(
+            num_scalar_prefetch=1,
+            grid=(cols // tile,),
+            in_specs=[
+                pl.BlockSpec((piece.shape[0], tile), lambda j, me: (0, j))
+                for _, _, piece in pieces
+            ],
+            out_specs=pl.BlockSpec((rows, tile), lambda j, me: (0, j)),
+        ),
+        cost_estimate=pl.CostEstimate(
+            flops=0, bytes_accessed=4 * rows * cols, transcendentals=0
+        ),
+        name="place_weight",
+    )(me.reshape(1), *[piece for _, _, piece in pieces])
+
+
+def gather_sc(weight, me):
+    size = weight.shape[0] // 8
+    mine = swap_y(lax.dynamic_slice_in_dim(weight, (me & 7) * size, size, 0))
+    count = lax.axis_size("dp")
+    groups = [[base + i for i in range(8)] for base in range(0, count, 8)]
+    return lax.all_gather(mine, "dp", axis_index_groups=groups, tiled=True)
+
+
+def relative_order(depth, me):
+    count = lax.axis_size("dp")
+    bits = count.bit_length() - 1
+    half = depth // count // 2
+    place = jnp.arange(depth, dtype=jnp.int32)
+    inner = place % half
+    order = place // half
+    which = (order >> (bits - 1)) & 1
+    rel = (order >> bits) & 1
+    for bit in range(1, bits):
+        rel = rel | (((order >> (bits - 1 - bit)) & 1) << bit)
+    source = (rel ^ me) * (2 * half) + which * half + inner
+    columns = lax.broadcasted_iota(jnp.int32, (depth, depth), 1)
+    return (columns == source[:, None]).astype(BF)
+
+
+def add(left, right):
+    return left.astype(F32) + right.astype(F32)
+
+
+def low_add(left, right):
+    return add(left, right).astype(BF)
+
+
+def finish(values, first_bit):
+    count = lax.axis_size("dp")
+    last = count.bit_length() - 2
+    for bit in range(first_bit, last + 1):
+        half = values.shape[0] // 2
+        got = swap(values[half:], bit)
+        values = (add if bit == last else low_add)(values[:half], got)
+    return values
+
+
+def reduce_grad(turned, own, other):
+    half = turned.shape[0] // 2
+    quarter = half // 2
+    kept = []
+    for side in (own, other):
+        got = swap(dg(turned[half:], side, 1, 0).astype(BF), 0)
+        kept.append((dg(turned[:half], side, 1, 0) + got.astype(F32)).astype(BF))
+    k_own, k_other = kept
+    eighth = quarter // 2
+    a_own = low_add(k_own[:eighth], swap(k_own[eighth:quarter], 1))
+    a_other = low_add(k_other[:eighth], swap(k_other[eighth:quarter], 1))
+    a_sum = low_add(a_own, swap_y(a_other))
+    b_sum = low_add(k_own[quarter:], swap_y(k_other[quarter:]))
+    return jnp.concatenate([finish(a_sum, 2), finish(b_sum, 1)], axis=0)
+
+
+def sum_everywhere(values):
+    count = lax.axis_size("dp")
+    for bit in range(count.bit_length() - 1):
+        values = values + swap(values, bit)
+    return values + swap_y(values)
+
+
+def stats(values):
+    center = values - jnp.mean(values, axis=-1, keepdims=True)
+    spread = jnp.mean(center * center, axis=-1, keepdims=True)
+    scale = lax.rsqrt(spread + EPSILON)
+    return center * scale, scale
+
+
+def norm_back(grad, normed, scale):
+    return scale * (
+        grad
+        - jnp.mean(grad, axis=-1, keepdims=True)
+        - normed * jnp.mean(grad * normed, axis=-1, keepdims=True)
+    )
+
+
+def paged(
+    tokens,
+    page_lengths,
+    qkv_weight,
+    qv_bias,
+    out_weight,
+    out_bias,
+    ln1_gain,
+    ln1_bias,
+    ff1_weight,
+    ff1_bias,
+    ff2_weight,
+    ff2_bias,
+    ln2_gain,
+    ln2_bias,
+    cotangent,
+):
+    row_count, depth = tokens.shape
+    share = row_count // 2
+    cols = qkv_weight.shape[2]
+    group = lax.axis_index("mp")
+    me = lax.axis_index("dp")
+    own_pages = page_lengths.shape[0] // 2
+
+    def own_rows(values, size):
+        return lax.dynamic_slice_in_dim(values, group * size, size, 0)
+
+    def in_order(own, other):
+        return jnp.where(
+            group == 0,
+            jnp.concatenate([own, other], axis=-1),
+            jnp.concatenate([other, own], axis=-1),
+        )
+
+    rows = own_rows(tokens, share)
+    cot = own_rows(cotangent, share).astype(F32)
+    lengths = own_rows(page_lengths, own_pages)
+
+    qkv_sides = (
+        qkv_weight,
+        gather_other(qkv_weight.reshape(3 * depth, cols), me).reshape(3, depth, cols),
+    )
+    qv_sides = (qv_bias, swap_y(qv_bias))
+    out_sides = (out_weight, gather_other(out_weight, me))
+    ff1_sides = (ff1_weight, gather_other(ff1_weight, me))
+    ff1b_sides = (ff1_bias, swap_y(ff1_bias))
+    ff2_sides = (ff2_weight, gather_other(ff2_weight, me))
+    order = relative_order(depth, me)
+
+    def turned(values):
+        return dg(order, values, 1, 1).astype(BF)
+
+    gain_one = ln1_gain.astype(F32)
+    gain_two = ln2_gain.astype(F32)
+
+    saved = []
+    attn = 0.0
+    for weight, bias, out_w in zip(qkv_sides, qv_sides, out_sides):
+        query = (dg(rows, weight[0], 1, 0) + bias[0].astype(F32)).astype(BF)
+        keyset = dg(rows, weight[1], 1, 0).astype(BF)
+        valueset = (dg(rows, weight[2], 1, 0) + bias[1].astype(F32)).astype(BF)
+        context, logsum = attn_fwd(lengths, query, keyset, valueset)
+        saved.append((query, keyset, valueset, logsum, context))
+        attn = attn + dg(context, out_w, 1, 0)
+    normed_one, scale_one = stats(rows.astype(F32) + attn + out_bias.astype(F32))
+    hidden = normed_one * gain_one + ln1_bias.astype(F32)
+    hidden_low = hidden.astype(BF)
+
+    acts = []
+    ffn = 0.0
+    for w_one, b_one, w_two in zip(ff1_sides, ff1b_sides, ff2_sides):
+        act, slope = ff1_gelu(hidden_low, w_one, b_one)
+        acts.append((act, slope))
+        ffn = ffn + dg(act, w_two, 1, 0)
+    normed_two, scale_two = stats(hidden + ffn + ff2_bias.astype(F32))
+    out_rows = (normed_two * gain_two + ln2_bias.astype(F32)).astype(BF)
+
+    dsecond = norm_back(cot * gain_two, normed_two, scale_two)
+    dffn = dsecond.astype(BF)
+    dgain_two = jnp.sum(cot * normed_two, axis=0)
+    dshift_two = jnp.sum(cot, axis=0)
+    dff2_bias = jnp.sum(dsecond, axis=0)
+    ff2_share = reduce_grad(turned(dffn), acts[0][0], acts[1][0])
+
+    dpres = []
+    dhid = 0.0
+    for (act, slope), w_one, w_two in zip(acts, ff1_sides, ff2_sides):
+        dpre = (dg(dffn, w_two, 1, 1) * slope.astype(F32)).astype(BF)
+        dpres.append(dpre)
+        dhid = dhid + dg(dpre, w_one, 1, 1)
+    ff1_share = reduce_grad(turned(hidden_low), dpres[0], dpres[1])
+    dff1_bias = in_order(*[jnp.sum(dpre.astype(F32), axis=0) for dpre in dpres])
+
+    dhidden = dsecond + dhid
+    dfirst = norm_back(dhidden * gain_one, normed_one, scale_one)
+    dattn = dfirst.astype(BF)
+    dgain_one = jnp.sum(dhidden * normed_one, axis=0)
+    dshift_one = jnp.sum(dhidden, axis=0)
+    dout_bias = jnp.sum(dfirst, axis=0)
+    out_share = reduce_grad(turned(dattn), saved[0][4], saved[1][4])
+
+    small = jnp.concatenate(
+        [dout_bias, dgain_one, dshift_one, dff1_bias, dff2_bias, dgain_two, dshift_two]
+    )
+    small = sum_everywhere(small.reshape(-1, 128)).reshape(-1)
+
+    grads = []
+    dtok = 0.0
+    for weight, out_w, (query, keyset, valueset, logsum, _) in zip(qkv_sides, out_sides, saved):
+        dctx = dg(dattn, out_w, 1, 1).astype(BF)
+        parts = attn_bwd(lengths, query, keyset, valueset, logsum, dctx)
+        grads.append(parts)
+        for t in range(3):
+            dtok = dtok + dg(parts[t], weight[t], 1, 1)
+    input_grad = (dfirst + dtok).astype(BF)
+    qkv_share = reduce_grad(
+        turned(rows), jnp.concatenate(grads[0], axis=1), jnp.concatenate(grads[1], axis=1)
+    )
+    qkv_share = jnp.stack([qkv_share[:, t * cols : (t + 1) * cols] for t in range(3)])
+    dqv = jnp.stack(
+        [
+            in_order(*[jnp.sum(parts[t].astype(F32), axis=0) for parts in grads])
+            for t in (0, 2)
+        ]
+    )
+    dqv = sum_everywhere(dqv.reshape(-1, 128)).reshape(2, -1)
+    ends = []
+    at = 0
+    for size in (depth, depth, depth, dff1_bias.shape[0], depth, depth, depth):
+        ends.append(small[at : at + size])
+        at += size
+    return (
+        out_rows,
+        input_grad,
+        qkv_share,
+        dqv,
+        out_share.T,
+        ends[0],
+        ends[1],
+        ends[2],
+        ff1_share,
+        ends[3],
+        ff2_share.T,
+        ends[4],
+        ends[5],
+        ends[6],
+    )
+
+
+def suits(mesh):
+    return mesh.shape["mp"] == 2 and mesh.shape["dp"] == 16
+
+
 def solution(mesh):
     in_specs = (
         P("dp", None),
@@ -256,4 +684,5 @@
         P(),
         P(),
     )
-    return jax.shard_map(local, mesh=mesh, in_specs=in_specs, out_specs=out_specs, check_vma=False)
+    body = paged if suits(mesh) else local
+    return jax.shard_map(body, mesh=mesh, in_specs=in_specs, out_specs=out_specs, check_vma=False)

time: 785 us -> 483 us (0.62)
  waiting for transfers between devices: 457 us -> 172 us
  starting transfers between devices: 1.2 us -> 84.7 us
  Pallas kernels: 0 us -> 69.8 us
  local copies, waits for them, and re-layouts: 70.2 us -> 26.2 us
  blocking collectives: 40.9 us -> 0 us
  other arithmetic: 51.3 us -> 13.5 us
  matrix products: 139 us -> 109 us
  between operations: 15.7 us -> 2.61 us
    reduce_scatter x4 -> x0, waiting for transfers between devices: 197 us -> none  [the longest x1 74.2 us: local(): lax.psum_scatter(dff2_weight.astype(jnp.bfloat16), 'dp', scatter_dimensio...]
    psum x3 -> x0, waiting for transfers between devices: 191 us -> none  [the longest x1 65.4 us: local(): attn = lax.psum(attn_part, 'mp').astype(jnp.float32)]
    ppermute x0 -> x96, waiting for transfers between devices: none -> 172 us  [the longest x80 111 us: swap(): return lax.ppermute(values, 'dp', [(i, i ^ 1 << bit) for i in range(count)])]
    ppermute x0 -> x96, starting transfers between devices: none -> 84.7 us  [the longest x80 65 us: swap(): return lax.ppermute(values, 'dp', [(i, i ^ 1 << bit) for i in range(count)])]
    pallas_call x0 -> x10, Pallas kernels: none -> 69.8 us  [the longest x2 20.9 us: attn_bwd(): pl.pallas_call(functools.partial(attn_bwd_body, seq=seq), out_shape=(jax....]
    unnamed x9 -> x0, waiting for transfers between devices: 68.9 us -> none
    psum x1 -> x0, blocking collectives: 40.9 us -> none  [local(): lax.psum((qv_placed, dout_bias, dgain_one, dshift_one, ff1_placed, dff2_b...]
    reduce_sum x14 -> x9, other arithmetic: 36.1 us -> 4.68 us  [the longest x1 1.85 us: paged(): dff2_bias = jnp.sum(dsecond, axis=0)]
  transfers between devices with their start and end apart: 8 -> 96, of which waited for: 8 -> 34; matrix products, arithmetic and copies ran while one was open for 6% -> 17% of each run, Pallas kernels for 0% -> 9%
where the time goes in v1:
time: 483 us; the launch traced here: 478 us
  waiting for transfers between devices  172 us (36%)
  matrix products  109 us (23%)
  starting transfers between devices  84.7 us (18%)
  Pallas kernels  69.8 us (14%)
  local copies, waits for them, and re-layouts  26.2 us (5%)
  other arithmetic  13.5 us (3%)
    ppermute x80, waiting for transfers between devices, swap(): return lax.ppermute(values, 'dp', [(i, i ^ 1 << bit) for i in range(count)])  111 us
    dot_general x42, matrix products, dg(): lax.dot_general(left, right, (((left_dim,), (right_dim,)), ((), ())), pre...  109 us
    ppermute x80, starting transfers between devices, swap(): return lax.ppermute(values, 'dp', [(i, i ^ 1 << bit) for i in range(count)])  65 us
    ppermute x16, waiting for transfers between devices, swap_y(): return lax.ppermute(values, 'mp', [(0, 1), (1, 0)])  61.1 us
    pallas_call x2, Pallas kernels, attn_bwd(): pl.pallas_call(functools.partial(attn_bwd_body, seq=seq), out_shape=(jax....  20.9 us
    ppermute x16, starting transfers between devices, swap_y(): return lax.ppermute(values, 'mp', [(0, 1), (1, 0)])  19.7 us
    pallas_call x4, Pallas kernels, gather_other(): pl.pallas_call(functools.partial(place_body, offsets=offsets), out_shape=...  18.1 us
    pallas_call x2, Pallas kernels, ff1_gelu(): pl.pallas_call(ff1_body, out_shape=(jax.ShapeDtypeStruct((rows, units), B...  15.4 us
  transfers between devices with their start and end apart: 96, of which 34 were waited for; matrix products, arithmetic and copies ran while one was open for 17% of the time, Pallas kernels for 9%

profile of v1, /device:TPU:0, one launch (start us, length us, event | category | flops | bytes accessed | tf_op | source)
XLA Modules:
  0.0 477.8 jit_solution(17983967990989374003)
XLA Ops:
  1.8 3.0 collective-permute-start
  7.7 3.1 fusion.20.q_ref
  10.7 6.0 %collective-permute-done.11.refs_0_ = bf16[64,1024]{1,0:T(8,128)(2,1)S(1)} collective-permute-done((bf16[64,1024]{1,0:T(8,128)(2,1)S(1)}, bf16[64,1024]{1,0:T(8,128)(2,1)S(1)}, u32[]{:S(2)}, u32[]{:S(2)}) %collective-permute-start.11) | collective-permute-done | bytes 131104 | tf_op jit(solution)/shard_map/ppermute | solution.py:377
  34.2 3.1 fusion.21.v_ref
  42.4 3.1 collective-permute-done.21.refs_0_
  47.6 7.8 %attn_fwd.2 = (bf16[512,512]{1,0:T(8,128)(2,1)}, f32[1,4,2,512]{3,2,1,0:T(2,128)}) custom-call(s32[1]{0:T(128)} %dynamic_slice.22.len_ref, bf16[512,512]{1,0:T(8,128)(2,1)} %fusion.20.q_ref, bf16[512,512]{1,0:T(8,128)(2,1)} %convolution_convert_fusion.11.k_ref, bf16[512,512]{1,0:T(8,128)(2,1)} %fusion.21.v_ref), custom_call_target="tpu_custom_call" | custom-call | flops 2147483648 | bytes 2097152 | tf_op jit(solution)/shard_map/attn_fwd/pallas_call | solution.py:265
  59.7 5.3 %collective-permute-done.3.refs_3_ = bf16[192,512]{1,0:T(8,128)(2,1)} collective-permute-done((bf16[192,512]{1,0:T(8,128)(2,1)}, bf16[192,512]{1,0:T(8,128)(2,1)}, u32[]{:S(2)}, u32[]{:S(2)}) %collective-permute-start.3) | collective-permute-done | bytes 196640 | tf_op jit(solution)/shard_map/ppermute | solution.py:373
  64.9 3.1 fusion.146
  68.7 4.4 collective-permute-done.4.refs_4_
  73.8 3.5 fusion.16
  78.6 3.3 place_weight.5
  90.4 3.5 place_weight.4
  93.9 3.2 convolution_convert_fusion.10.k_ref
  100.0 7.5 %attn_fwd.3 = (bf16[512,512]{1,0:T(8,128)(2,1)}, f32[1,4,2,512]{3,2,1,0:T(2,128)}) custom-call(s32[1]{0:T(128)} %dynamic_slice.22.len_ref, bf16[512,512]{1,0:T(8,128)(2,1)} %fusion.22.q_ref, bf16[512,512]{1,0:T(8,128)(2,1)} %convolution_convert_fusion.10.k_ref, bf16[512,512]{1,0:T(8,128)(2,1)} %fusion.23.v_ref), custom_call_target="tpu_custom_call" | custom-call | flops 2147483648 | bytes 2097152 | tf_op jit(solution)/shard_map/attn_fwd/pallas_call | solution.py:265
  107.6 3.2 fusion.144
  114.5 7.9 %ff1_gelu.2 = (bf16[512,2048]{1,0:T(8,128)(2,1)}, bf16[512,2048]{1,0:T(8,128)(2,1)}) custom-call(bf16[512,1024]{1,0:T(8,128)(2,1)} %fusion.15.h_ref, bf16[1024,2048]{1,0:T(8,128)(2,1)} %w_ref.1, bf16[1,2048]{1,0:T(2,128)(2,1)} %reshape.266.b_ref), custom_call_target="tpu_custom_call" | custom-call | flops 2147483648 | bytes 9437184 | tf_op jit(solution)/shard_map/ff1_gelu/pallas_call | solution.py:352
  123.7 6.6 %fusion.147 = f32[512,1024]{1,0:T(8,128)} fusion(bf16[512,2048]{1,0:T(8,128)(2,1)} %get-tuple-element.30, bf16[2048,1024]{1,0:T(8,128)(2,1)} %param.25), kind=kOutput, calls=%fused_computation.269 | convolution fusion | flops 2147483648 | bytes 8388608 | tf_op jit(solution)/shard_map/dot_general | solution.py:234
  133.8 6.6 %place_weight.6.w_ref = bf16[1024,2048]{1,0:T(8,128)(2,1)} custom-call(s32[1]{0:T(128)} %bitcast.5.me_ref, bf16[128,2048]{1,0:T(8,128)(2,1)} %collective-permute-done.21.refs_0_, bf16[128,2048]{1,0:T(8,128)(2,1)} %collective-permute-done.22.refs_1_, bf16[128,2048]{1,0:T(8,128)(2,1)} %collective-permute-done.23.refs_2_, bf16[64,2048]{1,0:T(8,128)(2,1)} %copy-done.35, ...), custom_call_target="tpu_custom_call" | custom-call | bytes 8388608 | tf_op jit(solution)/shard_map/place_weight/pallas_call | solution.py:401
  140.3 7.5 %ff1_gelu.3 = (bf16[512,2048]{1,0:T(8,128)(2,1)}, bf16[512,2048]{1,0:T(8,128)(2,1)}) custom-call(bf16[512,1024]{1,0:T(8,128)(2,1)} %fusion.15.h_ref, bf16[1024,2048]{1,0:T(8,128)(2,1)} %place_weight.6.w_ref, bf16[1,2048]{1,0:T(2,128)(2,1)} %reshape.267.b_ref), custom_call_target="tpu_custom_call" | custom-call | flops 2147483648 | bytes 9437184 | tf_op jit(solution)/shard_map/ff1_gelu/pallas_call | solution.py:352
  148.6 4.8 %place_weight.7 = bf16[2048,1024]{1,0:T(8,128)(2,1)} custom-call(s32[1]{0:T(128)} %bitcast.5.me_ref, bf16[256,1024]{1,0:T(8,128)(2,1)} %copy-done.31, bf16[256,1024]{1,0:T(8,128)(2,1)} %copy-done.23, bf16[256,1024]{1,0:T(8,128)(2,1)} %copy-done.24, bf16[128,1024]{1,0:T(8,128)(2,1)} %collective-permute-done.35.refs_3_, ...), custom_call_target="tpu_custom_call" | custom-call | bytes 8388608 | tf_op jit(solution)/shard_map/place_weight/pallas_call | solution.py:401
  153.4 6.1 %fusion.145 = (f32[512]{0:T(512)S(1)}, f32[512,1024]{1,0:T(8,128)S(1)}) fusion(f32[1024]{0:T(1024)S(1)} %convert_element_type.497, f32[512,1024]{1,0:T(8,128)} %fusion.147, bf16[512,2048]{1,0:T(8,128)(2,1)} %get-tuple-element.31, bf16[2048,1024]{1,0:T(8,128)(2,1)} %place_weight.7, f32[1024]{0:T(1024)S(1)} %convert_element_type.495, ...), kind=kOutput, calls=%fused_computation.267 | convolution fusion | flops 2151677440 | bytes 12601344 | tf_op jit(solution)/shard_map/dot_general | solution.py:234
  174.6 3.3 multiply_reduce_fusion
  182.3 10.5 %attn_bwd.3 = (bf16[512,512]{1,0:T(8,128)(2,1)}, bf16[512,512]{1,0:T(8,128)(2,1)}, bf16[512,512]{1,0:T(8,128)(2,1)}) custom-call(s32[1]{0:T(128)} %dynamic_slice.22.len_ref, bf16[512,512]{1,0:T(8,128)(2,1)} %fusion.22.q_ref, bf16[512,512]{1,0:T(8,128)(2,1)} %convolution_convert_fusion.10.k_ref, bf16[512,512]{1,0:T(8,128)(2,1)} %fusion.23.v_ref, ...), custom_call_target="tpu_custom_call" | custom-call | flops 5368709120 | bytes 3670016 | tf_op jit(solution)/shard_map/attn_bwd/pallas_call | solution.py:321
  192.7 3.5 fusion.41
  197.2 10.5 %attn_bwd.2 = (bf16[512,512]{1,0:T(8,128)(2,1)}, bf16[512,512]{1,0:T(8,128)(2,1)}, bf16[512,512]{1,0:T(8,128)(2,1)}) custom-call(s32[1]{0:T(128)} %dynamic_slice.22.len_ref, bf16[512,512]{1,0:T(8,128)(2,1)} %fusion.20.q_ref, bf16[512,512]{1,0:T(8,128)(2,1)} %convolution_convert_fusion.11.k_ref, bf16[512,512]{1,0:T(8,128)(2,1)} %fusion.21.v_ref, ...), custom_call_target="tpu_custom_call" | custom-call | flops 5368709120 | bytes 3670016 | tf_op jit(solution)/shard_map/attn_bwd/pallas_call | solution.py:321
  207.7 3.7 fusion.24
  228.0 3.3 fusion.38
  238.2 3.9 convolution_convert_fusion
  242.1 4.4 add_convert_fusion.8
  274.0 3.5 collective-permute-done.61
  285.0 4.5 collective-permute-done.66
  291.0 3.2 collective-permute-done.63
  295.7 2.9 collective-permute-done.67
  300.4 3.1 collective-permute-done.64
  305.2 3.1 collective-permute-done.68
  315.3 7.0 %collective-permute-done.45 = bf16[128,1536]{1,0:T(8,128)(2,1)S(1)} collective-permute-done((bf16[128,1536]{1,0:T(8,128)(2,1)S(1)}, bf16[128,1536]{1,0:T(8,128)(2,1)S(1)}, u32[]{:S(2)}, u32[]{:S(2)}) %collective-permute-start.45) | collective-permute-done | bytes 393248 | tf_op jit(solution)/shard_map/ppermute | solution.py:373
  334.6 17.2 %collective-permute-done.46 = bf16[128,1536]{1,0:T(8,128)(2,1)S(1)} collective-permute-done((bf16[128,1536]{1,0:T(8,128)(2,1)S(1)}, bf16[128,1536]{1,0:T(8,128)(2,1)S(1)}, u32[]{:S(2)}, u32[]{:S(2)}) %collective-permute-start.46) | collective-permute-done | bytes 393248 | tf_op jit(solution)/shard_map/ppermute | solution.py:377
  355.3 4.1 collective-permute-done.47
  361.7 24.8 %collective-permute-done.50 = bf16[128,1536]{1,0:T(8,128)(2,1)S(1)} collective-permute-done((bf16[128,1536]{1,0:T(8,128)(2,1)S(1)}, bf16[128,1536]{1,0:T(8,128)(2,1)S(1)}, u32[]{:S(2)}, u32[]{:S(2)}) %collective-permute-start.50) | collective-permute-done | bytes 393248 | tf_op jit(solution)/shard_map/ppermute | solution.py:373
  390.9 4.1 collective-permute-done.51
  397.3 4.4 collective-permute-done.52
  404.5 5.3 %collective-permute-done.78 = bf16[128,2048]{1,0:T(8,128)(2,1)S(1)} collective-permute-done((bf16[128,2048]{1,0:T(8,128)(2,1)S(1)}, bf16[128,2048]{1,0:T(8,128)(2,1)S(1)}, u32[]{:S(2)}, u32[]{:S(2)}) %collective-permute-start.78) | collective-permute-done | bytes 524320 | tf_op jit(solution)/shard_map/ppermute | solution.py:377
  411.8 9.3 %collective-permute-done.89 = bf16[128,2048]{1,0:T(8,128)(2,1)S(1)} collective-permute-done((bf16[128,2048]{1,0:T(8,128)(2,1)S(1)}, bf16[128,2048]{1,0:T(8,128)(2,1)S(1)}, u32[]{:S(2)}, u32[]{:S(2)}) %collective-permute-start.89) | collective-permute-done | bytes 524320 | tf_op jit(solution)/shard_map/ppermute | solution.py:377
  424.7 16.4 %collective-permute-done.92 = bf16[256,2048]{1,0:T(8,128)(2,1)S(1)} collective-permute-done((bf16[256,2048]{1,0:T(8,128)(2,1)S(1)}, bf16[256,2048]{1,0:T(8,128)(2,1)S(1)}, u32[]{:S(2)}, u32[]{:S(2)}) %collective-permute-start.92) | collective-permute-done | bytes 1048608 | tf_op jit(solution)/shard_map/ppermute | solution.py:377
  445.6 7.1 %collective-permute-done.80 = bf16[32,2048]{1,0:T(8,128)(2,1)S(1)} collective-permute-done((bf16[32,2048]{1,0:T(8,128)(2,1)S(1)}, bf16[32,2048]{1,0:T(8,128)(2,1)S(1)}, u32[]{:S(2)}, u32[]{:S(2)}) %collective-permute-start.80) | collective-permute-done | bytes 131104 | tf_op jit(solution)/shard_map/ppermute | solution.py:373
  456.8 8.4 %collective-permute-done.83 = bf16[64,2048]{1,0:T(8,128)(2,1)S(1)} collective-permute-done((bf16[64,2048]{1,0:T(8,128)(2,1)S(1)}, bf16[64,2048]{1,0:T(8,128)(2,1)S(1)}, u32[]{:S(2)}, u32[]{:S(2)}) %collective-permute-start.83) | collective-permute-done | bytes 262176 | tf_op jit(solution)/shard_map/ppermute | solution.py:373
  465.4 3.3 collective-permute-done.94
  468.9 6.2 %collective-permute-done.84 = bf16[32,2048]{1,0:T(8,128)(2,1)S(1)} collective-permute-done((bf16[32,2048]{1,0:T(8,128)(2,1)S(1)}, bf16[32,2048]{1,0:T(8,128)(2,1)S(1)}, u32[]{:S(2)}, u32[]{:S(2)}) %collective-permute-start.84) | collective-permute-done | bytes 131104 | tf_op jit(solution)/shard_map/ppermute | solution.py:373
  (494 shorter events, 192.0 us)
Async XLA Ops:
  1.8 18.3 %collective-permute-start = (bf16[384,512]{1,0:T(8,128)(2,1)S(1)}, bf16[384,512]{1,0:T(8,128)(2,1)}, u32[]{:S(2)}, u32[]{:S(2)}) collective-permute-start(bf16[384,512]{1,0:T(8,128)(2,1)S(1)} %constant_dynamic-slice_fusion.3), channel_id=1, source_target_pairs={{0,1},{1,0},{2,3},{3,2},{4,5},{5,4},{6,7},{7,6},{8,9},{9,8},{10,11... | collective-permute-start | bytes 1179656 | tf_op jit(solution)/shard_map/ppermute | solution.py:377
  4.8 21.9 %collective-permute-start.10 = (bf16[2,512]{1,0:T(2,128)(2,1)}, bf16[2,512]{1,0:T(2,128)(2,1)S(1)}, u32[]{:S(2)}, u32[]{:S(2)}) collective-permute-start(bf16[2,512]{1,0:T(2,128)(2,1)} %param.18), channel_id=1, source_target_pairs={{0,1},{1,0},{2,3},{3,2},{4,5},{5,4},{6,7},{7,6},{8,9},{9,8},{10,11... | collective-permute-start | bytes 6152 | tf_op jit(solution)/shard_map/ppermute | solution.py:377
  20.1 17.5 %collective-permute-start.2 = (bf16[384,512]{1,0:T(8,128)(2,1)}, bf16[384,512]{1,0:T(8,128)(2,1)S(1)}, u32[]{:S(2)}, u32[]{:S(2)}) collective-permute-start(bf16[384,512]{1,0:T(8,128)(2,1)} %collective-permute-done.refs_0_), channel_id=1, source_target_pairs={{0,8},{2,10},{4,12},{6,14},{8,0},{10,2},{12,4},{14,6},{16,24},{18,... | collective-permute-start | bytes 1179656 | tf_op jit(solution)/shard_map/ppermute | solution.py:373
  30.5 15.0 %collective-permute-start.21 = (bf16[128,2048]{1,0:T(8,128)(2,1)S(1)}, bf16[128,2048]{1,0:T(8,128)(2,1)}, u32[]{:S(2)}, u32[]{:S(2)}) collective-permute-start(bf16[128,2048]{1,0:T(8,128)(2,1)S(1)} %constant_dynamic-slice_fusion.1), channel_id=1, source_target_pairs={{0,1},{1,0},{2,3},{3,2},{4,5},{5,4},{6,7},{7,6},{8,9},{9,8},{10,11... | collective-permute-start | bytes 1572872 | tf_op jit(solution)/shard_map/ppermute | solution.py:377
  31.2 24.9 %collective-permute-start.32 = (bf16[256,1024]{1,0:T(8,128)(2,1)S(1)}, bf16[256,1024]{1,0:T(8,128)(2,1)S(1)}, u32[]{:S(2)}, u32[]{:S(2)}) collective-permute-start(bf16[256,1024]{1,0:T(8,128)(2,1)S(1)} %constant_dynamic-slice_fusion), channel_id=1, source_target_pairs={{0,1},{1,0},{2,3},{3,2},{4,5},{5,4},{6,7},{7,6},{8,9},{9,8},{10,11... | collective-permute-start | bytes 1572872 | tf_op jit(solution)/shard_map/ppermute | solution.py:377
  33.4 13.7 %collective-permute-start.1 = (bf16[384,512]{1,0:T(8,128)(2,1)}, bf16[384,512]{1,0:T(8,128)(2,1)S(1)}, u32[]{:S(2)}, u32[]{:S(2)}) collective-permute-start(bf16[384,512]{1,0:T(8,128)(2,1)} %collective-permute-done.refs_0_), channel_id=1, source_target_pairs={{0,4},{2,6},{4,0},{6,2},{8,12},{10,14},{12,8},{14,10},{16,20},{18,... | collective-permute-start | bytes 1179656 | tf_op jit(solution)/shard_map/ppermute | solution.py:373
  42.1 15.6 %collective-permute-start.20 = (bf16[32,1024]{1,0:T(8,128)(2,1)}, bf16[32,1024]{1,0:T(8,128)(2,1)}, u32[]{:S(2)}, u32[]{:S(2)}) collective-permute-start(bf16[32,1024]{1,0:T(8,128)(2,1)} %collective-permute-done.15.refs_4_), channel_id=1, source_target_pairs={{0,2},{2,0},{4,6},{6,4},{8,10},{10,8},{12,14},{14,12},{16,18},{18,... | collective-permute-start | bytes 196616 | tf_op jit(solution)/shard_map/ppermute | solution.py:373
  45.5 27.6 %collective-permute-start.22 = (bf16[128,2048]{1,0:T(8,128)(2,1)}, bf16[128,2048]{1,0:T(8,128)(2,1)}, u32[]{:S(2)}, u32[]{:S(2)}) collective-permute-start(bf16[128,2048]{1,0:T(8,128)(2,1)} %collective-permute-done.21.refs_0_), channel_id=1, source_target_pairs={{0,4},{2,6},{4,0},{6,2},{8,12},{10,14},{12,8},{14,10},{16,20},{18,... | collective-permute-start | bytes 1572872 | tf_op jit(solution)/shard_map/ppermute | solution.py:373
  47.0 26.7 %collective-permute-start.23 = (bf16[128,2048]{1,0:T(8,128)(2,1)}, bf16[128,2048]{1,0:T(8,128)(2,1)}, u32[]{:S(2)}, u32[]{:S(2)}) collective-permute-start(bf16[128,2048]{1,0:T(8,128)(2,1)} %collective-permute-done.21.refs_0_), channel_id=1, source_target_pairs={{0,8},{2,10},{4,12},{6,14},{8,0},{10,2},{12,4},{14,6},{16,24},{18,... | collective-permute-start | bytes 1572872 | tf_op jit(solution)/shard_map/ppermute | solution.py:373
  47.1 17.9 %collective-permute-start.3 = (bf16[192,512]{1,0:T(8,128)(2,1)}, bf16[192,512]{1,0:T(8,128)(2,1)}, u32[]{:S(2)}, u32[]{:S(2)}) collective-permute-start(bf16[192,512]{1,0:T(8,128)(2,1)} %slice.445), channel_id=1, source_target_pairs={{0,4},{2,6},{4,0},{6,2},{8,12},{10,14},{12,8},{14,10},{16,20},{18,... | collective-permute-start | bytes 589832 | tf_op jit(solution)/shard_map/ppermute | solution.py:373
  56.2 21.1 %collective-permute-start.33 = (bf16[256,1024]{1,0:T(8,128)(2,1)S(1)}, bf16[256,1024]{1,0:T(8,128)(2,1)S(1)}, u32[]{:S(2)}, u32[]{:S(2)}) collective-permute-start(bf16[256,1024]{1,0:T(8,128)(2,1)S(1)} %collective-permute-done.32.refs_0_), channel_id=1, source_target_pairs={{0,4},{2,6},{4,0},{6,2},{8,12},{10,14},{12,8},{14,10},{16,20},{18,... | collective-permute-start | bytes 1572872 | tf_op jit(solution)/shard_map/ppermute | solution.py:373
  57.7 20.1 %collective-permute-start.34 = (bf16[256,1024]{1,0:T(8,128)(2,1)S(1)}, bf16[256,1024]{1,0:T(8,128)(2,1)S(1)}, u32[]{:S(2)}, u32[]{:S(2)}) collective-permute-start(bf16[256,1024]{1,0:T(8,128)(2,1)S(1)} %collective-permute-done.32.refs_0_), channel_id=1, source_target_pairs={{0,8},{2,10},{4,12},{6,14},{8,0},{10,2},{12,4},{14,6},{16,24},{18,... | collective-permute-start | bytes 1572872 | tf_op jit(solution)/shard_map/ppermute | solution.py:373
  73.2 13.5 %collective-permute-start.5 = (bf16[384,512]{1,0:T(8,128)(2,1)}, bf16[384,512]{1,0:T(8,128)(2,1)}, u32[]{:S(2)}, u32[]{:S(2)}) collective-permute-start(bf16[384,512]{1,0:T(8,128)(2,1)} %collective-permute-done.refs_0_), channel_id=1, source_target_pairs={{0,2},{2,0},{4,6},{6,4},{8,10},{10,8},{12,14},{14,12},{16,18},{18,... | collective-permute-start | bytes 1179656 | tf_op jit(solution)/shard_map/ppermute | solution.py:373
  73.2 13.9 %collective-permute-start.6 = (bf16[384,512]{1,0:T(8,128)(2,1)S(1)}, bf16[384,512]{1,0:T(8,128)(2,1)}, u32[]{:S(2)}, u32[]{:S(2)}) collective-permute-start(bf16[384,512]{1,0:T(8,128)(2,1)S(1)} %collective-permute-done.1.refs_1_), channel_id=1, source_target_pairs={{0,2},{2,0},{4,6},{6,4},{8,10},{10,8},{12,14},{14,12},{16,18},{18,... | collective-permute-start | bytes 1179656 | tf_op jit(solution)/shard_map/ppermute | solution.py:373
  73.7 14.3 %collective-permute-start.7 = (bf16[384,512]{1,0:T(8,128)(2,1)S(1)}, bf16[384,512]{1,0:T(8,128)(2,1)}, u32[]{:S(2)}, u32[]{:S(2)}) collective-permute-start(bf16[384,512]{1,0:T(8,128)(2,1)S(1)} %collective-permute-done.2.refs_2_), channel_id=1, source_target_pairs={{0,2},{2,0},{4,6},{6,4},{8,10},{10,8},{12,14},{14,12},{16,18},{18,... | collective-permute-start | bytes 1179656 | tf_op jit(solution)/shard_map/ppermute | solution.py:373
  86.7 24.5 %collective-permute-start.26 = (bf16[128,2048]{1,0:T(8,128)(2,1)}, bf16[128,2048]{1,0:T(8,128)(2,1)}, u32[]{:S(2)}, u32[]{:S(2)}) collective-permute-start(bf16[128,2048]{1,0:T(8,128)(2,1)} %collective-permute-done.21.refs_0_), channel_id=1, source_target_pairs={{0,2},{2,0},{4,6},{6,4},{8,10},{10,8},{12,14},{14,12},{16,18},{18,... | collective-permute-start | bytes 1572872 | tf_op jit(solution)/shard_map/ppermute | solution.py:373
  87.1 25.6 %collective-permute-start.24 = (bf16[64,2048]{1,0:T(8,128)(2,1)}, bf16[64,2048]{1,0:T(8,128)(2,1)S(1)}, u32[]{:S(2)}, u32[]{:S(2)}) collective-permute-start(bf16[64,2048]{1,0:T(8,128)(2,1)} %slice.454), channel_id=1, source_target_pairs={{0,4},{2,6},{4,0},{6,2},{8,12},{10,14},{12,8},{14,10},{16,20},{18,... | collective-permute-start | bytes 786440 | tf_op jit(solution)/shard_map/ppermute | solution.py:373
  87.9 34.5 %collective-permute-start.25 = (bf16[64,2048]{1,0:T(8,128)(2,1)}, bf16[64,2048]{1,0:T(8,128)(2,1)}, u32[]{:S(2)}, u32[]{:S(2)}) collective-permute-start(bf16[64,2048]{1,0:T(8,128)(2,1)} %slice.455), channel_id=1, source_target_pairs={{0,8},{2,10},{4,12},{6,14},{8,0},{10,2},{12,4},{14,6},{16,24},{18,... | collective-permute-start | bytes 786440 | tf_op jit(solution)/shard_map/ppermute | solution.py:373
  89.2 33.9 %collective-permute-start.27 = (bf16[128,2048]{1,0:T(8,128)(2,1)}, bf16[128,2048]{1,0:T(8,128)(2,1)}, u32[]{:S(2)}, u32[]{:S(2)}) collective-permute-start(bf16[128,2048]{1,0:T(8,128)(2,1)} %collective-permute-done.22.refs_1_), channel_id=1, source_target_pairs={{0,2},{2,0},{4,6},{6,4},{8,10},{10,8},{12,14},{14,12},{16,18},{18,... | collective-permute-start | bytes 1572872 | tf_op jit(solution)/shard_map/ppermute | solution.py:373
  89.9 33.7 %collective-permute-start.28 = (bf16[128,2048]{1,0:T(8,128)(2,1)}, bf16[128,2048]{1,0:T(8,128)(2,1)}, u32[]{:S(2)}, u32[]{:S(2)}) collective-permute-start(bf16[128,2048]{1,0:T(8,128)(2,1)} %collective-permute-done.23.refs_2_), channel_id=1, source_target_pairs={{0,2},{2,0},{4,6},{6,4},{8,10},{10,8},{12,14},{14,12},{16,18},{18,... | collective-permute-start | bytes 1572872 | tf_op jit(solution)/shard_map/ppermute | solution.py:373
  122.5 25.4 %collective-permute-start.37 = (bf16[256,1024]{1,0:T(8,128)(2,1)}, bf16[256,1024]{1,0:T(8,128)(2,1)}, u32[]{:S(2)}, u32[]{:S(2)}) collective-permute-start(bf16[256,1024]{1,0:T(8,128)(2,1)} %copy-done.31), channel_id=1, source_target_pairs={{0,2},{2,0},{4,6},{6,4},{8,10},{10,8},{12,14},{14,12},{16,18},{18,... | collective-permute-start | bytes 1572872 | tf_op jit(solution)/shard_map/ppermute | solution.py:373
  122.6 25.3 %collective-permute-start.38 = (bf16[256,1024]{1,0:T(8,128)(2,1)}, bf16[256,1024]{1,0:T(8,128)(2,1)}, u32[]{:S(2)}, u32[]{:S(2)}) collective-permute-start(bf16[256,1024]{1,0:T(8,128)(2,1)} %copy-done.23), channel_id=1, source_target_pairs={{0,2},{2,0},{4,6},{6,4},{8,10},{10,8},{12,14},{14,12},{16,18},{18,... | collective-permute-start | bytes 1572872 | tf_op jit(solution)/shard_map/ppermute | solution.py:373
  123.0 24.8 %collective-permute-start.39 = (bf16[256,1024]{1,0:T(8,128)(2,1)}, bf16[256,1024]{1,0:T(8,128)(2,1)}, u32[]{:S(2)}, u32[]{:S(2)}) collective-permute-start(bf16[256,1024]{1,0:T(8,128)(2,1)} %copy-done.24), channel_id=1, source_target_pairs={{0,2},{2,0},{4,6},{6,4},{8,10},{10,8},{12,14},{14,12},{16,18},{18,... | collective-permute-start | bytes 1572872 | tf_op jit(solution)/shard_map/ppermute | solution.py:373
  130.9 16.9 %collective-permute-start.40 = (bf16[128,1024]{1,0:T(8,128)(2,1)}, bf16[128,1024]{1,0:T(8,128)(2,1)S(1)}, u32[]{:S(2)}, u32[]{:S(2)}) collective-permute-start(bf16[128,1024]{1,0:T(8,128)(2,1)} %collective-permute-done.35.refs_3_), channel_id=1, source_target_pairs={{0,2},{2,0},{4,6},{6,4},{8,10},{10,8},{12,14},{14,12},{16,18},{18,... | collective-permute-start | bytes 786440 | tf_op jit(solution)/shard_map/ppermute | solution.py:373
  131.4 16.5 %collective-permute-start.41 = (bf16[128,1024]{1,0:T(8,128)(2,1)}, bf16[128,1024]{1,0:T(8,128)(2,1)}, u32[]{:S(2)}, u32[]{:S(2)}) collective-permute-start(bf16[128,1024]{1,0:T(8,128)(2,1)} %collective-permute-done.36.refs_4_), channel_id=1, source_target_pairs={{0,2},{2,0},{4,6},{6,4},{8,10},{10,8},{12,14},{14,12},{16,18},{18,... | collective-permute-start | bytes 786440 | tf_op jit(solution)/shard_map/ppermute | solution.py:373
  234.9 12.8 %collective-permute-start.53 = (f32[16,128]{1,0:T(8,128)S(1)}, f32[16,128]{1,0:T(8,128)S(1)}, u32[]{:S(2)}, u32[]{:S(2)}) collective-permute-start(f32[16,128]{1,0:T(8,128)S(1)} %reshape.268), channel_id=1, source_target_pairs={{0,2},{2,0},{4,6},{6,4},{8,10},{10,8},{12,14},{14,12},{16,18},{18,... | collective-permute-start | bytes 24584 | tf_op jit(solution)/shard_map/ppermute | solution.py:373
  250.0 58.3 %collective-permute-start.44 = (bf16[512,1536]{1,0:T(8,128)(2,1)}, bf16[512,1536]{1,0:T(8,128)(2,1)}, u32[]{:S(2)}, u32[]{:S(2)}) collective-permute-start(bf16[512,1536]{1,0:T(8,128)(2,1)} %convolution_convert_fusion), channel_id=1, source_target_pairs={{0,2},{2,0},{4,6},{6,4},{8,10},{10,8},{12,14},{14,12},{16,18},{18,... | collective-permute-start | bytes 4718600 | tf_op jit(solution)/shard_map/ppermute | solution.py:373
  266.7 45.3 %collective-permute-start.42 = (bf16[512,1536]{1,0:T(8,128)(2,1)}, bf16[512,1536]{1,0:T(8,128)(2,1)}, u32[]{:S(2)}, u32[]{:S(2)}) collective-permute-start(bf16[512,1536]{1,0:T(8,128)(2,1)} %convolution_convert_fusion.1), channel_id=1, source_target_pairs={{0,2},{2,0},{4,6},{6,4},{8,10},{10,8},{12,14},{14,12},{16,18},{18,... | collective-permute-start | bytes 4718600 | tf_op jit(solution)/shard_map/ppermute | solution.py:373
  267.8 55.0 %collective-permute-start.76 = (bf16[512,2048]{1,0:T(8,128)(2,1)}, bf16[512,2048]{1,0:T(8,128)(2,1)S(1)}, u32[]{:S(2)}, u32[]{:S(2)}) collective-permute-start(bf16[512,2048]{1,0:T(8,128)(2,1)} %convolution_convert_fusion.4), channel_id=1, source_target_pairs={{0,2},{2,0},{4,6},{6,4},{8,10},{10,8},{12,14},{14,12},{16,18},{18,... | collective-permute-start | bytes 6291464 | tf_op jit(solution)/shard_map/ppermute | solution.py:373
  282.4 42.8 %collective-permute-start.87 = (bf16[512,2048]{1,0:T(8,128)(2,1)S(1)}, bf16[512,2048]{1,0:T(8,128)(2,1)S(1)}, u32[]{:S(2)}, u32[]{:S(2)}) collective-permute-start(bf16[512,2048]{1,0:T(8,128)(2,1)S(1)} %copy-done.57), channel_id=1, source_target_pairs={{0,2},{2,0},{4,6},{6,4},{8,10},{10,8},{12,14},{14,12},{16,18},{18,... | collective-permute-start | bytes 6291464 | tf_op jit(solution)/shard_map/ppermute | solution.py:373
  308.2 20.1 %collective-permute-start.74 = (bf16[512,2048]{1,0:T(8,128)(2,1)S(1)}, bf16[512,2048]{1,0:T(8,128)(2,1)S(1)}, u32[]{:S(2)}, u32[]{:S(2)}) collective-permute-start(bf16[512,2048]{1,0:T(8,128)(2,1)S(1)} %copy-done.56), channel_id=1, source_target_pairs={{0,2},{2,0},{4,6},{6,4},{8,10},{10,8},{12,14},{14,12},{16,18},{18,... | collective-permute-start | bytes 6291464 | tf_op jit(solution)/shard_map/ppermute | solution.py:373
  312.3 18.8 %collective-permute-start.85 = (bf16[512,2048]{1,0:T(8,128)(2,1)S(1)}, bf16[512,2048]{1,0:T(8,128)(2,1)S(1)}, u32[]{:S(2)}, u32[]{:S(2)}) collective-permute-start(bf16[512,2048]{1,0:T(8,128)(2,1)S(1)} %copy-done.55), channel_id=1, source_target_pairs={{0,2},{2,0},{4,6},{6,4},{8,10},{10,8},{12,14},{14,12},{16,18},{18,... | collective-permute-start | bytes 6291464 | tf_op jit(solution)/shard_map/ppermute | solution.py:373
  322.9 30.8 %collective-permute-start.49 = (bf16[256,1536]{1,0:T(8,128)(2,1)S(1)}, bf16[256,1536]{1,0:T(8,128)(2,1)S(1)}, u32[]{:S(2)}, u32[]{:S(2)}) collective-permute-start(bf16[256,1536]{1,0:T(8,128)(2,1)S(1)} %slice.469), channel_id=1, source_target_pairs={{0,1},{1,0},{2,3},{3,2},{4,5},{5,4},{6,7},{7,6},{8,9},{9,8},{10,11... | collective-permute-start | bytes 2359304 | tf_op jit(solution)/shard_map/ppermute | solution.py:377
  325.3 26.6 %collective-permute-start.46 = (bf16[128,1536]{1,0:T(8,128)(2,1)S(1)}, bf16[128,1536]{1,0:T(8,128)(2,1)S(1)}, u32[]{:S(2)}, u32[]{:S(2)}) collective-permute-start(bf16[128,1536]{1,0:T(8,128)(2,1)S(1)} %add_convert_fusion.23), channel_id=1, source_target_pairs={{0,1},{1,0},{2,3},{3,2},{4,5},{5,4},{6,7},{7,6},{8,9},{9,8},{10,11... | collective-permute-start | bytes 1179656 | tf_op jit(solution)/shard_map/ppermute | solution.py:377
  328.4 94.9 %collective-permute-start.81 = (bf16[256,2048]{1,0:T(8,128)(2,1)S(1)}, bf16[256,2048]{1,0:T(8,128)(2,1)S(1)}, u32[]{:S(2)}, u32[]{:S(2)}) collective-permute-start(bf16[256,2048]{1,0:T(8,128)(2,1)S(1)} %slice.512), channel_id=1, source_target_pairs={{0,1},{1,0},{2,3},{3,2},{4,5},{5,4},{6,7},{7,6},{8,9},{9,8},{10,11... | collective-permute-start | bytes 3145736 | tf_op jit(solution)/shard_map/ppermute | solution.py:377
  331.1 28.7 %collective-permute-start.77 = (bf16[128,2048]{1,0:T(8,128)(2,1)S(1)}, bf16[128,2048]{1,0:T(8,128)(2,1)S(1)}, u32[]{:S(2)}, u32[]{:S(2)}) collective-permute-start(bf16[128,2048]{1,0:T(8,128)(2,1)S(1)} %slice.506), channel_id=1, source_target_pairs={{0,4},{2,6},{4,0},{6,2},{8,12},{10,14},{12,8},{14,10},{16,20},{18,... | collective-permute-start | bytes 1572872 | tf_op jit(solution)/shard_map/ppermute | solution.py:373
  334.2 69.4 %collective-permute-start.75 = (bf16[128,2048]{1,0:T(8,128)(2,1)S(1)}, bf16[128,2048]{1,0:T(8,128)(2,1)S(1)}, u32[]{:S(2)}, u32[]{:S(2)}) collective-permute-start(bf16[128,2048]{1,0:T(8,128)(2,1)S(1)} %slice.504), channel_id=1, source_target_pairs={{0,4},{2,6},{4,0},{6,2},{8,12},{10,14},{12,8},{14,10},{16,20},{18,... | collective-permute-start | bytes 1572872 | tf_op jit(solution)/shard_map/ppermute | solution.py:373
  351.8 36.8 %collective-permute-start.88 = (bf16[128,2048]{1,0:T(8,128)(2,1)S(1)}, bf16[128,2048]{1,0:T(8,128)(2,1)S(1)}, u32[]{:S(2)}, u32[]{:S(2)}) collective-permute-start(bf16[128,2048]{1,0:T(8,128)(2,1)S(1)} %slice.525), channel_id=1, source_target_pairs={{0,4},{2,6},{4,0},{6,2},{8,12},{10,14},{12,8},{14,10},{16,20},{18,... | collective-permute-start | bytes 1572872 | tf_op jit(solution)/shard_map/ppermute | solution.py:373
  359.4 52.4 %collective-permute-start.86 = (bf16[128,2048]{1,0:T(8,128)(2,1)S(1)}, bf16[128,2048]{1,0:T(8,128)(2,1)S(1)}, u32[]{:S(2)}, u32[]{:S(2)}) collective-permute-start(bf16[128,2048]{1,0:T(8,128)(2,1)S(1)} %slice.523), channel_id=1, source_target_pairs={{0,4},{2,6},{4,0},{6,2},{8,12},{10,14},{12,8},{14,10},{16,20},{18,... | collective-permute-start | bytes 1572872 | tf_op jit(solution)/shard_map/ppermute | solution.py:373
  359.9 26.6 %collective-permute-start.50 = (bf16[128,1536]{1,0:T(8,128)(2,1)S(1)}, bf16[128,1536]{1,0:T(8,128)(2,1)S(1)}, u32[]{:S(2)}, u32[]{:S(2)}) collective-permute-start(bf16[128,1536]{1,0:T(8,128)(2,1)S(1)} %slice.471), channel_id=1, source_target_pairs={{0,4},{2,6},{4,0},{6,2},{8,12},{10,14},{12,8},{14,10},{16,20},{18,... | collective-permute-start | bytes 1179656 | tf_op jit(solution)/shard_map/ppermute | solution.py:373
  395.0 14.9 %collective-permute-start.78 = (bf16[128,2048]{1,0:T(8,128)(2,1)S(1)}, bf16[128,2048]{1,0:T(8,128)(2,1)S(1)}, u32[]{:S(2)}, u32[]{:S(2)}) collective-permute-start(bf16[128,2048]{1,0:T(8,128)(2,1)S(1)} %add_convert_fusion.17), channel_id=1, source_target_pairs={{0,1},{1,0},{2,3},{3,2},{4,5},{5,4},{6,7},{7,6},{8,9},{9,8},{10,11... | collective-permute-start | bytes 1572872 | tf_op jit(solution)/shard_map/ppermute | solution.py:377
  401.7 19.5 %collective-permute-start.89 = (bf16[128,2048]{1,0:T(8,128)(2,1)S(1)}, bf16[128,2048]{1,0:T(8,128)(2,1)S(1)}, u32[]{:S(2)}, u32[]{:S(2)}) collective-permute-start(bf16[128,2048]{1,0:T(8,128)(2,1)S(1)} %add_convert_fusion.13), channel_id=1, source_target_pairs={{0,1},{1,0},{2,3},{3,2},{4,5},{5,4},{6,7},{7,6},{8,9},{9,8},{10,11... | collective-permute-start | bytes 1572872 | tf_op jit(solution)/shard_map/ppermute | solution.py:377
  403.5 37.5 %collective-permute-start.92 = (bf16[256,2048]{1,0:T(8,128)(2,1)S(1)}, bf16[256,2048]{1,0:T(8,128)(2,1)S(1)}, u32[]{:S(2)}, u32[]{:S(2)}) collective-permute-start(bf16[256,2048]{1,0:T(8,128)(2,1)S(1)} %slice.531), channel_id=1, source_target_pairs={{0,1},{1,0},{2,3},{3,2},{4,5},{5,4},{6,7},{7,6},{8,9},{9,8},{10,11... | collective-permute-start | bytes 3145736 | tf_op jit(solution)/shard_map/ppermute | solution.py:377
  410.2 32.2 %collective-permute-start.79 = (bf16[64,2048]{1,0:T(8,128)(2,1)S(1)}, bf16[64,2048]{1,0:T(8,128)(2,1)S(1)}, u32[]{:S(2)}, u32[]{:S(2)}) collective-permute-start(bf16[64,2048]{1,0:T(8,128)(2,1)S(1)} %slice.508), channel_id=1, source_target_pairs={{0,8},{2,10},{4,12},{6,14},{8,0},{10,2},{12,4},{14,6},{16,24},{18,... | collective-permute-start | bytes 786440 | tf_op jit(solution)/shard_map/ppermute | solution.py:373
  421.7 21.3 %collective-permute-start.90 = (bf16[64,2048]{1,0:T(8,128)(2,1)S(1)}, bf16[64,2048]{1,0:T(8,128)(2,1)S(1)}, u32[]{:S(2)}, u32[]{:S(2)}) collective-permute-start(bf16[64,2048]{1,0:T(8,128)(2,1)S(1)} %slice.527), channel_id=1, source_target_pairs={{0,8},{2,10},{4,12},{6,14},{8,0},{10,2},{12,4},{14,6},{16,24},{18,... | collective-permute-start | bytes 786440 | tf_op jit(solution)/shard_map/ppermute | solution.py:373
  423.8 30.6 %collective-permute-start.82 = (bf16[128,2048]{1,0:T(8,128)(2,1)S(1)}, bf16[128,2048]{1,0:T(8,128)(2,1)S(1)}, u32[]{:S(2)}, u32[]{:S(2)}) collective-permute-start(bf16[128,2048]{1,0:T(8,128)(2,1)S(1)} %slice.514), channel_id=1, source_target_pairs={{0,4},{2,6},{4,0},{6,2},{8,12},{10,14},{12,8},{14,10},{16,20},{18,... | collective-permute-start | bytes 1572872 | tf_op jit(solution)/shard_map/ppermute | solution.py:373
  441.5 13.0 %collective-permute-start.93 = (bf16[128,2048]{1,0:T(8,128)(2,1)S(1)}, bf16[128,2048]{1,0:T(8,128)(2,1)S(1)}, u32[]{:S(2)}, u32[]{:S(2)}) collective-permute-start(bf16[128,2048]{1,0:T(8,128)(2,1)S(1)} %slice.533), channel_id=1, source_target_pairs={{0,4},{2,6},{4,0},{6,2},{8,12},{10,14},{12,8},{14,10},{16,20},{18,... | collective-permute-start | bytes 1572872 | tf_op jit(solution)/shard_map/ppermute | solution.py:373
  454.7 14.0 %collective-permute-start.94 = (bf16[64,2048]{1,0:T(8,128)(2,1)S(1)}, bf16[64,2048]{1,0:T(8,128)(2,1)S(1)}, u32[]{:S(2)}, u32[]{:S(2)}) collective-permute-start(bf16[64,2048]{1,0:T(8,128)(2,1)S(1)} %slice.535), channel_id=1, source_target_pairs={{0,8},{2,10},{4,12},{6,14},{8,0},{10,2},{12,4},{14,6},{16,24},{18,... | collective-permute-start | bytes 786440 | tf_op jit(solution)/shard_map/ppermute | solution.py:373
  (127 other events, 959.5 us)
